TPU v7x, 128 devices: a whole 4x4x4 slice. The times are simulated.
128 devices in a mesh: req: 32 (over x, y, z_hi), rep: 4 (over z_lo, core).
Axes of the slice: x: 4, y: 4, z: 4 (z_hi: 2, z_lo: 2; z = z_hi * 2 + z_lo), core: 2. Of those that a mesh axis runs over, the one named last changes fastest.
Arguments:
- tokens: bfloat16 [128, 2, 2048], P('req'), may hold values from -6 to 6
- norm_gains: float32 [2, 2048], replicated, may hold values from 0.1 to 1.9
- w_kv: bfloat16 [2048, 2, 2048], P(None, None, 'rep'), may hold values from -0.125 to 0.125
- w_query: bfloat16 [32, 2048, 512], P('req', None, 'rep'), may hold values from -0.125 to 0.125
- w_out: bfloat16 [32, 512, 2048], P('req', 'rep'), may hold values from -0.5 to 0.5
- w_gate: bfloat16 [32, 2048, 1408], P('req', None, 'rep'), may hold values from -0.125 to 0.125
- w_up: bfloat16 [32, 2048, 1408], P('req', None, 'rep'), may hold values from -0.125 to 0.125
- w_down: bfloat16 [32, 1408, 2048], P('req', 'rep'), may hold values from -0.078125 to 0.078125
- kv_pages: bfloat16 [8192, 16, 2, 2048], P('req', None, None, 'rep'), may hold values from -80 to 80
- page_table: int32 [128, 64], P('req'), may hold values from 0 to 255, as said below
- cache_len: int32 [128], P('req'), may hold values from 1 to 1024
- route_ids: int32 [128, 2, 2, 2], P('req'), may hold values from 0 to 7, all different within a row
- route_gates: bfloat16 [128, 2, 2, 2], P('req'), may hold values from 0.19921875 to 1
- new_slot: int32 [128], P('req'), may hold values from 0 to 127, each once
Outputs:
- layer_out: bfloat16 [128, 2, 2048], P('req')
Inputs may be any that keep to these rules, and one draw needn't show every extreme that they name: `page_table`: row i lists 64 distinct pages of the pool of the device that holds request i; two requests of one device share no page.
All inputs are finite; a program needn't handle non-finite values.
Results may differ from a plain program's by a relative error of at most 0.022.
Values may be sent and summed in bfloat16 or wider, within the bound.
No kernel may reach another device: no remote copies, remote signals or barrier semaphores. Data moves between devices by JAX's collectives and lax.ppermute only.
A program may use at most 128 MiB of HBM per device.

v0:
```python
import math
import jax
import jax.numpy as jnp
from jax import lax
from jax.sharding import PartitionSpec as P

HD = 128
EXPERTS = 8
EPSILON = 1e-06
MASKED = -1e30


def normalize(values, gain_row):
    scaling = lax.rsqrt(jnp.mean(values * values, axis=-1, keepdims=True) + EPSILON)
    return (values * scaling * gain_row).astype(jnp.bfloat16)


def expert_share(ids_block, gates_block, expert):
    return jnp.sum(jnp.where(ids_block == expert, gates_block.astype(jnp.float32), 0.0), axis=-1)


def attend(queries, cache_keys, cache_values, lengths, extra_keys, extra_values, extra_live):
    inv_scale = 1.0 / math.sqrt(queries.shape[-1])
    cache_scores = (
        jnp.einsum("jskhc,jlhc->jskhl", queries, cache_keys, preferred_element_type=jnp.float32)
        * inv_scale
    )
    alive_mask = jnp.arange(cache_keys.shape[1], dtype=jnp.int32)[None, :] < lengths[:, None]
    cache_scores = jnp.where(alive_mask[:, None, None, None, :], cache_scores, MASKED)
    extra_scores = (
        jnp.einsum("jskhc,jxhc->jskhx", queries, extra_keys, preferred_element_type=jnp.float32)
        * inv_scale
    )
    extra_scores = jnp.where(extra_live[None, :, None, None, :], extra_scores, MASKED)
    highest = jnp.maximum(jnp.max(cache_scores, axis=-1), jnp.max(extra_scores, axis=-1))[..., None]
    cache_exp = jnp.exp(cache_scores - highest)
    extra_exp = jnp.exp(extra_scores - highest)
    denominator = (jnp.sum(cache_exp, axis=-1) + jnp.sum(extra_exp, axis=-1))[..., None]
    cache_weight = (cache_exp / denominator).astype(jnp.bfloat16)
    extra_weight = (extra_exp / denominator).astype(jnp.bfloat16)
    mixture = jnp.einsum(
        "jskhl,jlhc->jskhc", cache_weight, cache_values, preferred_element_type=jnp.float32
    )
    mixture = mixture + jnp.einsum(
        "jskhx,jxhc->jskhc", extra_weight, extra_values, preferred_element_type=jnp.float32
    )
    return mixture.astype(jnp.bfloat16)


def combine(term_fn, all_rows):
    partial_value = lax.psum_scatter(
        term_fn(jnp.int32(0), all_rows // lax.axis_size("req") * lax.axis_size("req")).astype(
            jnp.bfloat16
        ),
        "req",
        scatter_dimension=0,
        tiled=True,
    )
    return lax.psum(partial_value, "rep").astype(jnp.float32)


def shards(
    tokens,
    norm_gains,
    w_kv,
    w_query,
    w_out,
    w_gate,
    w_up,
    w_down,
    kv_pages,
    page_table,
    cache_len,
    route_ids,
    route_gates,
    new_slot,
):
    rows_dev = tokens.shape[0]
    req_count = lax.axis_size("req")
    all_rows = rows_dev * req_count
    holders = req_count // EXPERTS
    expert = lax.axis_index("req") // holders
    head_dim = HD
    heads_rep = kv_pages.shape[-1] // head_dim
    heads_dev = w_query.shape[-1] // head_dim
    inputs = tokens.astype(jnp.float32)
    normed = normalize(inputs, norm_gains[0])
    cache_pages = kv_pages[page_table].reshape(rows_dev, -1, 2, heads_rep, head_dim)
    cache_keys = cache_pages[:, :, 0]
    cache_values = cache_pages[:, :, 1]
    experts_row = jnp.arange(EXPERTS, dtype=jnp.int32)

    def fresh_kv(normed_rows):
        return jnp.einsum(
            "jd,dtc->jtc", normed_rows, w_kv, preferred_element_type=jnp.float32
        ).astype(jnp.bfloat16)

    def pair_kv(first_kv, second_kv):
        return jnp.stack([first_kv, second_kv], axis=1).reshape(rows_dev, 2, 2, heads_rep, head_dim)

    first_fresh = fresh_kv(normed[:, 0])

    def section(step_list, gathered, slot_map, all_ids, all_gates, extra_kv):
        step_count = len(step_list)
        first_step = step_list[0]
        step_span = slice(first_step, first_step + step_count)
        inverse = (
            jnp.zeros((all_rows,), jnp.int32)
            .at[slot_map]
            .set(jnp.arange(all_rows, dtype=jnp.int32))
        )
        queries = jnp.einsum(
            "bsd,dc->bsc", gathered, w_query[0], preferred_element_type=jnp.float32
        ).astype(jnp.bfloat16)
        columns = []
        own_ids = []
        for position, current in enumerate(step_list):
            if current == 0:
                columns.append(queries[:, position])
                own_ids.append(route_ids[:, 0, 0])
            else:
                columns.append(jnp.take(queries[:, position], slot_map, axis=0))
                own_ids.append(jnp.take(all_ids[:, 0, 1], new_slot, axis=0))
        ordered = jnp.stack(columns, axis=1).reshape(
            req_count, rows_dev, step_count, heads_dev * head_dim
        )
        arrived = lax.all_to_all(ordered, "req", split_axis=0, concat_axis=0, tiled=True)
        arrived = arrived.reshape(EXPERTS, holders, rows_dev, step_count, heads_dev, head_dim)
        chosen = (jnp.stack(own_ids, axis=1)[..., None] == experts_row).astype(jnp.bfloat16)
        picked = jnp.einsum(
            "jske,egjshc->jskghc", chosen, arrived, preferred_element_type=jnp.float32
        ).astype(jnp.bfloat16)
        picked = picked.reshape(rows_dev, step_count, 2, heads_rep, head_dim)
        extra_live = jnp.array(
            [[extra_slot <= current for extra_slot in range(2)] for current in step_list]
        )
        result = attend(
            picked,
            cache_keys,
            cache_values,
            cache_len,
            extra_kv[:, :, 0],
            extra_kv[:, :, 1],
            extra_live,
        )
        result = result.reshape(rows_dev, step_count, 2, holders, heads_dev, head_dim)
        spread = jnp.einsum(
            "jske,jskghc->egjshc", chosen, result, preferred_element_type=jnp.float32
        ).astype(jnp.bfloat16)
        returned = lax.all_to_all(
            spread.reshape(req_count, rows_dev, step_count, heads_dev * head_dim),
            "req",
            split_axis=0,
            concat_axis=0,
            tiled=True,
        )
        returned = returned.reshape(all_rows, step_count, heads_dev * head_dim)
        answers = jnp.stack(
            [
                (
                    returned[:, position]
                    if current == 0
                    else jnp.take(returned[:, position], inverse, axis=0)
                )
                for position, current in enumerate(step_list)
            ],
            axis=1,
        )
        attn_share = expert_share(all_ids[:, 0, step_span], all_gates[:, 0, step_span], expert)
        ffn_share = expert_share(all_ids[:, 1, step_span], all_gates[:, 1, step_span], expert)

        def attn_term(first_row, row_count):
            return (
                jnp.einsum("bsc,cd->bsd", answers, w_out[0], preferred_element_type=jnp.float32)
                * attn_share[..., None]
            )

        hidden = inputs[:, step_span] + combine(attn_term, all_rows)
        hidden_normed = normalize(hidden, norm_gains[1])
        block_rows = lax.all_gather(hidden_normed, "req", axis=0, tiled=True)
        gate_part = jnp.einsum(
            "bsd,df->bsf", block_rows, w_gate[0], preferred_element_type=jnp.float32
        )
        up_part = jnp.einsum("bsd,df->bsf", block_rows, w_up[0], preferred_element_type=jnp.float32)
        hidden_units = (jax.nn.silu(gate_part) * up_part).astype(jnp.bfloat16)

        def ffn_term(first_row, row_count):
            return (
                jnp.einsum(
                    "bsf,fd->bsd", hidden_units, w_down[0], preferred_element_type=jnp.float32
                )
                * ffn_share[..., None]
            )

        return (hidden + combine(ffn_term, all_rows)).astype(jnp.bfloat16)

    first_rows, all_ids, all_gates, slot_map = (
        lax.all_gather(normed[:, 0:1], "req", axis=0, tiled=True),
        lax.all_gather(route_ids, "req", axis=0, tiled=True),
        lax.all_gather(route_gates, "req", axis=0, tiled=True),
        lax.all_gather(new_slot, "req", axis=0, tiled=True),
    )
    early = section(
        (0,), first_rows, slot_map, all_ids, all_gates, pair_kv(first_fresh, first_fresh)
    )
    second_rows = lax.all_gather(normed[:, 1:2], "req", axis=0, tiled=True)
    second_fresh = fresh_kv(jnp.take(second_rows[:, 0], new_slot, axis=0))
    later = section(
        (1,), second_rows, slot_map, all_ids, all_gates, pair_kv(first_fresh, second_fresh)
    )
    return jnp.concatenate([early, later], axis=1)


def solution(mesh):
    in_specs = (
        P("req", None, None),
        P(),
        P(None, None, "rep"),
        P("req", None, "rep"),
        P("req", "rep", None),
        P("req", None, "rep"),
        P("req", None, "rep"),
        P("req", "rep", None),
        P("req", None, None, "rep"),
        P("req", None),
        P("req"),
        P("req", None, None, None),
        P("req", None, None, None),
        P("req"),
    )
    out_specs = P("req", None, None)
    return jax.shard_map(shards, mesh=mesh, in_specs=in_specs, out_specs=out_specs, check_vma=False)
```

profile of v0, /device:TPU:1, one launch (start us, length us, event | category | flops | bytes accessed | tf_op | source)
XLA Modules:
  0.0 1477.4 jit_solution(3638717455090007884)
XLA Ops:
  9.2 88.1 %all_gather.21 = bf16[128,1,2048]{2,1,0:T(2,128)(2,1)S(1)} all-gather(bf16[4,1,2048]{2,1,0:T(2,128)(2,1)S(1)} %copy.217), channel_id=1, replica_groups=mesh['req'=32,'rep'=4] {'req'}, dimensions={0}, use_global_device_ids=true | all-gather | bytes 540672 | tf_op jit(solution)/shard_map/all_gather | solution.py:198
  99.4 3.9 all-to-all-start
  107.6 16.5 %all-reduce = s32[128]{0:T(128)S(1)} all-reduce(s32[128]{0:T(128)S(1)} %dynamic-update-slice), channel_id=1, replica_groups=mesh['req'=32,'rep'=4] {'req'}, use_global_device_ids=true, to_apply=%add | all-reduce | flops 128 | bytes 1024
  132.9 76.8 %all_gather.23 = bf16[128,2,2,2]{3,2,1,0:T(2,128)(2,1)S(1)} all-gather(bf16[4,2,2,2]{3,2,1,0:T(2,128)(2,1)S(1)} %copy.235), channel_id=1, replica_groups=mesh['req'=32,'rep'=4] {'req'}, dimensions={0}, use_global_device_ids=true | all-gather | bytes 2112 | tf_op jit(solution)/shard_map/all_gather | solution.py:200
  210.5 75.0 %all_gather.22 = s32[128,2,2,2]{3,2,1,0:T(2,128)S(1)} all-gather(s32[4,2,2,2]{3,2,1,0:T(2,128)S(1)} %copy.233), channel_id=1, replica_groups=mesh['req'=32,'rep'=4] {'req'}, dimensions={0}, use_global_device_ids=true | all-gather | bytes 4224 | tf_op jit(solution)/shard_map/all_gather | solution.py:199
  286.4 82.6 %all_gather.25 = bf16[128,1,2048]{2,1,0:T(2,128)(2,1)S(1)} all-gather(bf16[4,1,2048]{2,1,0:T(2,128)(2,1)S(1)} %copy.241), channel_id=1, replica_groups=mesh['req'=32,'rep'=4] {'req'}, dimensions={0}, use_global_device_ids=true | all-gather | bytes 540672 | tf_op jit(solution)/shard_map/all_gather | solution.py:206
  373.7 25.4 %gather_fusion = bf16[256,16,2,512]{3,2,1,0:T(2,128)(2,1)} fusion(bf16[256,16,2,512]{3,2,1,0:T(2,128)(2,1)} %param.26, s32[1024]{0:T(1024)S(1)} %pad_clamp_fusion.3), kind=kCustom, calls=%fused_computation.2 | custom fusion | bytes 16778240 | tf_op jit(solution)/shard_map/gather | solution.py:88
  399.1 14.0 reshape.554
  413.1 8.1 fusion.151
  423.4 4.0 all-to-all-start.2
  427.8 8.1 all-to-all-done.2
  443.3 3.7 fusion.1
  451.7 3.9 all-to-all-start.3
  458.7 5.5 all-to-all-done.3
  464.2 4.6 all-to-all-start.1
  470.7 6.6 all-to-all-done.1
  482.9 388.7 %all-reduce.14.cloned.1.call-done = (bf16[128,1,2048]{2,0,1:T(8,128)(2,1)}, bf16[128,1,2048]{2,0,1:T(8,128)(2,1)}) async-done(((bf16[128,1,2048]{2,0,1:T(8,128)(2,1)}, bf16[128,1,2048]{2,0,1:T(8,128)(2,1)}), (bf16[128,1,2048]{2,0,1:T(8,128)(2,1)}, bf16[128,1,2048]{2,0,1:T(8,128)(2,1)})) %all-reduce.14.cloned.1.call-update) | async-done | bytes 1048592
  873.1 32.1 %all-reduce.8 = (bf16[4,1,2048]{2,0,1:T(4,128)(2,1)S(1)}, bf16[4,1,2048]{2,0,1:T(4,128)(2,1)S(1)}) all-reduce(bf16[4,1,2048]{2,0,1:T(4,128)(2,1)S(1)} %constant_dynamic-slice_fusion.3, bf16[4,1,2048]{2,0,1:T(4,128)(2,1)S(1)} %constant_dynamic-slice_fusion.1), channel_id=1, replica_groups=mesh['req'=32,'rep'=4] {'rep'}, use_global_device_ids=true, to_apply=%region_7.8 | all-reduce | flops 16384 | bytes 65536 | tf_op jit(solution)/shard_map/psum | solution.py:59
  905.5 87.1 %all_gather.27 = bf16[128,1,2048]{2,1,0:T(2,128)(2,1)S(1)} all-gather(bf16[4,1,2048]{2,1,0:T(2,128)(2,1)S(1)} %copy.258), channel_id=1, replica_groups=mesh['req'=32,'rep'=4] {'req'}, dimensions={0}, use_global_device_ids=true | all-gather | bytes 540672 | tf_op jit(solution)/shard_map/all_gather | solution.py:180
  992.7 79.9 %all_gather.24 = bf16[128,1,2048]{2,1,0:T(2,128)(2,1)S(1)} all-gather(bf16[4,1,2048]{2,1,0:T(2,128)(2,1)S(1)} %copy.237), channel_id=1, replica_groups=mesh['req'=32,'rep'=4] {'req'}, dimensions={0}, use_global_device_ids=true | all-gather | bytes 540672 | tf_op jit(solution)/shard_map/all_gather | solution.py:180
  1074.0 4.1 fusion.12
  1078.0 3.7 fusion.14
  1081.7 354.5 %all-reduce.12.cloned.1.call-done = (bf16[128,1,2048]{2,0,1:T(8,128)(2,1)}, bf16[128,1,2048]{2,0,1:T(8,128)(2,1)}) async-done(((bf16[128,1,2048]{2,0,1:T(8,128)(2,1)}, bf16[128,1,2048]{2,0,1:T(8,128)(2,1)}), (bf16[128,1,2048]{2,0,1:T(8,128)(2,1)}, bf16[128,1,2048]{2,0,1:T(8,128)(2,1)})) %all-reduce.12.cloned.1.call-update) | async-done | bytes 1048592
  1437.7 32.1 %all-reduce.7 = (bf16[4,1,2048]{2,0,1:T(4,128)(2,1)S(1)}, bf16[4,1,2048]{2,0,1:T(4,128)(2,1)S(1)}) all-reduce(bf16[4,1,2048]{2,0,1:T(4,128)(2,1)S(1)} %constant_dynamic-slice_fusion, bf16[4,1,2048]{2,0,1:T(4,128)(2,1)S(1)} %constant_dynamic-slice_fusion.2), channel_id=1, replica_groups=mesh['req'=32,'rep'=4] {'rep'}, use_global_device_ids=true, to_apply=%region_23.25 | all-reduce | flops 16384 | bytes 65536 | tf_op jit(solution)/shard_map/psum | solution.py:59
  (138 shorter events, 53.3 us)
Async XLA Ops:
  6.5 1067.4 %copy-start = (bf16[1,352,2048]{2,1,0:T(8,128)(2,1)S(1)}, bf16[1,352,2048]{2,1,0:T(8,128)(2,1)}, u32[]{:S(2)}) copy-start(bf16[1,352,2048]{2,1,0:T(8,128)(2,1)} %param.25) | copy-start | bytes 4325380
  99.4 324.0 %all-to-all-start = ((bf16[32,4,1,128]{3,1,2,0:T(4,128)(2,1)}), bf16[32,4,1,128]{3,1,2,0:T(4,128)(2,1)S(1)}, u32[]{:S(2)}, u32[]{:S(2)}) async-start(bf16[32,4,1,128]{3,1,2,0:T(4,128)(2,1)} %bitcast.8), calls=%async_computation | async-start | bytes 65536 | tf_op jit(solution)/shard_map/all_to_all | solution.py:127
  129.2 240.1 %copy-start.8 = (bf16[1,2048,128]{2,1,0:T(8,128)(2,1)S(1)}, bf16[1,2048,128]{2,1,0:T(8,128)(2,1)}, u32[]{:S(2)}) copy-start(bf16[1,2048,128]{2,1,0:T(8,128)(2,1)} %param.21) | copy-start | bytes 1572868
  370.8 65.1 %copy-start.14 = (s32[4,2]{1,0:T(4,128)}, s32[4,2]{1,0:T(4,128)S(1)}, u32[]{:S(2)}) copy-start(s32[4,2]{1,0:T(4,128)S(1)} %broadcast_select_fusion.1) | copy-start | bytes 100
  423.4 16.4 %copy-start.13 = (s32[4,2]{1,0:T(4,128)}, s32[4,2]{1,0:T(4,128)S(1)}, u32[]{:S(2)}) copy-start(s32[4,2]{1,0:T(4,128)S(1)} %copy.216) | copy-start | bytes 100
  423.4 25.2 %copy-start.10 = (bf16[4,1,2,4,128]{4,1,3,0,2:T(2,128)(2,1)}, bf16[4,1,2,4,128]{4,1,3,0,2:T(2,128)(2,1)S(1)}, u32[]{:S(2)}) copy-start(bf16[4,1,2,4,128]{4,1,3,0,2:T(2,128)(2,1)S(1)} %stack.20) | copy-start | bytes 24580
  423.4 17.6 %copy-start.11 = (bf16[4,1,2,4,128]{4,1,3,0,2:T(2,128)(2,1)}, bf16[4,1,2,4,128]{4,1,3,0,2:T(2,128)(2,1)S(1)}, u32[]{:S(2)}) copy-start(bf16[4,1,2,4,128]{4,1,3,0,2:T(2,128)(2,1)S(1)} %stack.19) | copy-start | bytes 24580
  423.4 12.5 all-to-all-start.2
  435.9 3.8 copy-start.6
  439.7 2.1 copy-start.12
  443.3 3.7 copy-start.5
  447.1 1.5 copy-start.15
  447.1 30.3 %copy-start.7 = (bf16[1,128,2048]{2,1,0:T(8,128)(2,1)S(1)}, bf16[1,128,2048]{2,1,0:T(8,128)(2,1)}, u32[]{:S(2)}) copy-start(bf16[1,128,2048]{2,1,0:T(8,128)(2,1)} %param.22) | copy-start | bytes 1572868
  448.5 34.4 %copy-start.9 = (bf16[4,2,2048]{2,1,0:T(2,128)(2,1)S(1)}, bf16[4,2,2048]{2,1,0:T(2,128)(2,1)}, u32[]{:S(2)}) copy-start(bf16[4,2,2048]{2,1,0:T(2,128)(2,1)} %param.18) | copy-start | bytes 98308
  448.5 624.1 %copy-start.1 = (bf16[1,2048,352]{1,2,0:T(8,128)(2,1)S(1)}, bf16[1,2048,352]{1,2,0:T(8,128)(2,1)}, u32[]{:S(2)}) copy-start(bf16[1,2048,352]{1,2,0:T(8,128)(2,1)} %param.23) | copy-start | bytes 4325380
  451.7 12.5 all-to-all-start.3
  464.2 13.2 all-to-all-start.1
  468.8 402.8 %all-reduce.14.cloned.1.call-start = ((), (), s32[]{:S(2)}) async-start(), calls=%async_computation.5 | async-start | bytes 2097152
  481.2 955.0 %all-reduce.12.cloned.1.call-start = ((), (), s32[]{:S(2)}) async-start(), calls=%async_computation.4 | async-start | bytes 2097152
  992.7 81.3 %copy-start.4 = (bf16[128,1,2048]{2,1,0:T(2,128)(2,1)}, bf16[128,1,2048]{2,1,0:T(2,128)(2,1)S(1)}, u32[]{:S(2)}) copy-start(bf16[128,1,2048]{2,1,0:T(2,128)(2,1)S(1)} %all_gather.27) | copy-start | bytes 1572868
  1072.6 1.3 copy-start.2
  1073.9 4.1 copy-start.3
Sparse Core Ops, SparseCore 0:
  481.3 390.2 all-reduce.13
  1081.8 354.3 all-reduce.11
where the time goes:
time: 1480 us
  waiting for transfers between devices  763 us (52%)
  blocking collectives  570 us (39%)
  local copies, waits for them, and re-layouts  67.3 us (5%)
  matrix products  35 us (2%)
  starting transfers between devices  16.4 us (1%)
  between operations  15.1 us (1%)
    unnamed x4, waiting for transfers between devices  743 us
    all_gather x2, blocking collectives, section(): block_rows = lax.all_gather(hidden_normed, 'req', axis=0, tiled=True)  167 us
    all_gather x1, blocking collectives, shards(): lax.all_gather(normed[:, 0:1], 'req', axis=0, tiled=True)  88.1 us
    all_gather x1, blocking collectives, shards(): second_rows = lax.all_gather(normed[:, 1:2], 'req', axis=0, tiled=True)  82.6 us
    all_gather x1, blocking collectives, shards(): lax.all_gather(route_gates, 'req', axis=0, tiled=True)  76.8 us
    all_gather x1, blocking collectives, shards(): lax.all_gather(route_ids, 'req', axis=0, tiled=True)  75 us
    psum x2, blocking collectives, combine(): return lax.psum(partial_value, 'rep').astype(jnp.float32)  64.1 us
  transfers between devices with their start and end apart: 6, of which 5 were waited for; matrix products, arithmetic and copies ran while one was open for 5% of the time, Pallas kernels for 0%

commit v1 on v0

--- a/solution.py
+++ b/solution.py
@@ -203,7 +203,9 @@
     early = section(
         (0,), first_rows, slot_map, all_ids, all_gates, pair_kv(first_fresh, first_fresh)
     )
-    second_rows = lax.all_gather(normed[:, 1:2], "req", axis=0, tiled=True)
+    second_rows = jnp.concatenate(
+        lax.all_to_all(jnp.stack([normed[:, 1:2]] * lax.axis_size("req")), "req", 0, 0), axis=0
+    )
     second_fresh = fresh_kv(jnp.take(second_rows[:, 0], new_slot, axis=0))
     later = section(
         (1,), second_rows, slot_map, all_ids, all_gates, pair_kv(first_fresh, second_fresh)

time: 1480 us -> 1390 us (0.939)
  blocking collectives: 570 us -> 488 us
  waiting for transfers between devices: 763 us -> 744 us
    all_gather x1 -> x0, blocking collectives: 82.6 us -> none  [shards(): second_rows = lax.all_gather(normed[:, 1:2], 'req', axis=0, tiled=True)]
  transfers between devices with their start and end apart: 6 -> 7, of which waited for: 5 -> 5; matrix products, arithmetic and copies ran while one was open for 5% -> 6% of each run, Pallas kernels for 0% -> 0%
where the time goes in v1:
time: 1390 us
  waiting for transfers between devices  744 us (54%)
  blocking collectives  488 us (35%)
  local copies, waits for them, and re-layouts  68.5 us (5%)
  matrix products  37.1 us (3%)
  starting transfers between devices  29 us (2%)
  between operations  15.1 us (1%)
    unnamed x4, waiting for transfers between devices  730 us
    all_gather x2, blocking collectives, section(): block_rows = lax.all_gather(hidden_normed, 'req', axis=0, tiled=True)  167 us
    all_gather x1, blocking collectives, shards(): lax.all_gather(normed[:, 0:1], 'req', axis=0, tiled=True)  88.1 us
    all_gather x1, blocking collectives, shards(): lax.all_gather(route_gates, 'req', axis=0, tiled=True)  76.8 us
    all_gather x1, blocking collectives, shards(): lax.all_gather(route_ids, 'req', axis=0, tiled=True)  75 us
    psum x2, blocking collectives, combine(): return lax.psum(partial_value, 'rep').astype(jnp.float32)  64.1 us
  transfers between devices with their start and end apart: 7, of which 5 were waited for; matrix products, arithmetic and copies ran while one was open for 6% of the time, Pallas kernels for 0%

profile of v1, /device:TPU:1, one launch (start us, length us, event | category | flops | bytes accessed | tf_op | source)
XLA Modules:
  0.0 1390.4 jit_solution(17143646481162760606)
XLA Ops:
  9.2 88.1 %all_gather.18 = bf16[128,1,2048]{2,1,0:T(2,128)(2,1)S(1)} all-gather(bf16[4,1,2048]{2,1,0:T(2,128)(2,1)S(1)} %copy.214), channel_id=1, replica_groups=mesh['req'=32,'rep'=4] {'req'}, dimensions={0}, use_global_device_ids=true | all-gather | bytes 540672 | tf_op jit(solution)/shard_map/all_gather | solution.py:198
  99.4 3.9 all-to-all-start
  107.6 16.5 %all-reduce = s32[128]{0:T(128)S(1)} all-reduce(s32[128]{0:T(128)S(1)} %dynamic-update-slice), channel_id=1, replica_groups=mesh['req'=32,'rep'=4] {'req'}, use_global_device_ids=true, to_apply=%add | all-reduce | flops 128 | bytes 1024
  132.3 76.8 %all_gather.20 = bf16[128,2,2,2]{3,2,1,0:T(2,128)(2,1)S(1)} all-gather(bf16[4,2,2,2]{3,2,1,0:T(2,128)(2,1)S(1)} %copy.232), channel_id=1, replica_groups=mesh['req'=32,'rep'=4] {'req'}, dimensions={0}, use_global_device_ids=true | all-gather | bytes 2112 | tf_op jit(solution)/shard_map/all_gather | solution.py:200
  209.9 75.0 %all_gather.19 = s32[128,2,2,2]{3,2,1,0:T(2,128)S(1)} all-gather(s32[4,2,2,2]{3,2,1,0:T(2,128)S(1)} %copy.230), channel_id=1, replica_groups=mesh['req'=32,'rep'=4] {'req'}, dimensions={0}, use_global_device_ids=true | all-gather | bytes 4224 | tf_op jit(solution)/shard_map/all_gather | solution.py:199
  285.8 25.4 %gather_fusion = bf16[256,16,2,512]{3,2,1,0:T(2,128)(2,1)} fusion(bf16[256,16,2,512]{3,2,1,0:T(2,128)(2,1)} %param.26, s32[1024]{0:T(1024)S(1)} %pad_clamp_fusion.3), kind=kCustom, calls=%fused_computation.2 | custom fusion | bytes 16778240 | tf_op jit(solution)/shard_map/gather | solution.py:88
  311.2 14.0 %reshape.559 = bf16[4,1024,2,4,128]{4,3,2,1,0:T(4,128)(2,1)} reshape(bf16[256,16,2,512]{3,2,1,0:T(2,128)(2,1)} %gather_fusion) | data formatting | bytes 16777216 | tf_op jit(solution)/shard_map/reshape | solution.py:88
  325.2 8.1 fusion.151
  335.8 4.5 all-to-all-start.2
  340.8 3.5 fusion.156
  353.7 7.4 all-to-all-start.3
  364.1 5.5 all-to-all-done.3
  369.6 3.9 all-to-all-start.1
  378.2 3.6 fusion
  386.2 9.2 all-to-all-start.4
  397.4 6.7 all-to-all-done.4
  409.1 375.6 %all-reduce.14.cloned.1.call-done = (bf16[128,1,2048]{2,0,1:T(8,128)(2,1)}, bf16[128,1,2048]{2,0,1:T(8,128)(2,1)}) async-done(((bf16[128,1,2048]{2,0,1:T(8,128)(2,1)}, bf16[128,1,2048]{2,0,1:T(8,128)(2,1)}), (bf16[128,1,2048]{2,0,1:T(8,128)(2,1)}, bf16[128,1,2048]{2,0,1:T(8,128)(2,1)})) %all-reduce.14.cloned.1.call-update) | async-done | bytes 1048592
  786.2 32.1 %all-reduce.8 = (bf16[4,1,2048]{2,0,1:T(4,128)(2,1)S(1)}, bf16[4,1,2048]{2,0,1:T(4,128)(2,1)S(1)}) all-reduce(bf16[4,1,2048]{2,0,1:T(4,128)(2,1)S(1)} %constant_dynamic-slice_fusion.3, bf16[4,1,2048]{2,0,1:T(4,128)(2,1)S(1)} %constant_dynamic-slice_fusion.1), channel_id=1, replica_groups=mesh['req'=32,'rep'=4] {'rep'}, use_global_device_ids=true, to_apply=%region_7.8 | all-reduce | flops 16384 | bytes 65536 | tf_op jit(solution)/shard_map/psum | solution.py:59
  818.6 87.1 %all_gather.23 = bf16[128,1,2048]{2,1,0:T(2,128)(2,1)S(1)} all-gather(bf16[4,1,2048]{2,1,0:T(2,128)(2,1)S(1)} %copy.254), channel_id=1, replica_groups=mesh['req'=32,'rep'=4] {'req'}, dimensions={0}, use_global_device_ids=true | all-gather | bytes 540672 | tf_op jit(solution)/shard_map/all_gather | solution.py:180
  905.7 79.9 %all_gather.21 = bf16[128,1,2048]{2,1,0:T(2,128)(2,1)S(1)} all-gather(bf16[4,1,2048]{2,1,0:T(2,128)(2,1)S(1)} %copy.234), channel_id=1, replica_groups=mesh['req'=32,'rep'=4] {'req'}, dimensions={0}, use_global_device_ids=true | all-gather | bytes 540672 | tf_op jit(solution)/shard_map/all_gather | solution.py:180
  987.0 4.1 fusion.12
  991.1 3.7 fusion.14
  994.8 354.5 %all-reduce.12.cloned.1.call-done = (bf16[128,1,2048]{2,0,1:T(8,128)(2,1)}, bf16[128,1,2048]{2,0,1:T(8,128)(2,1)}) async-done(((bf16[128,1,2048]{2,0,1:T(8,128)(2,1)}, bf16[128,1,2048]{2,0,1:T(8,128)(2,1)}), (bf16[128,1,2048]{2,0,1:T(8,128)(2,1)}, bf16[128,1,2048]{2,0,1:T(8,128)(2,1)})) %all-reduce.12.cloned.1.call-update) | async-done | bytes 1048592
  1350.8 32.1 %all-reduce.7 = (bf16[4,1,2048]{2,0,1:T(4,128)(2,1)S(1)}, bf16[4,1,2048]{2,0,1:T(4,128)(2,1)S(1)}) all-reduce(bf16[4,1,2048]{2,0,1:T(4,128)(2,1)S(1)} %constant_dynamic-slice_fusion, bf16[4,1,2048]{2,0,1:T(4,128)(2,1)S(1)} %constant_dynamic-slice_fusion.2), channel_id=1, replica_groups=mesh['req'=32,'rep'=4] {'rep'}, use_global_device_ids=true, to_apply=%region_23.25 | all-reduce | flops 16384 | bytes 65536 | tf_op jit(solution)/shard_map/psum | solution.py:59
  (133 shorter events, 54.2 us)
Async XLA Ops:
  6.5 980.5 %copy-start = (bf16[1,352,2048]{2,1,0:T(8,128)(2,1)S(1)}, bf16[1,352,2048]{2,1,0:T(8,128)(2,1)}, u32[]{:S(2)}) copy-start(bf16[1,352,2048]{2,1,0:T(8,128)(2,1)} %param.25) | copy-start | bytes 4325380
  99.4 235.3 %all-to-all-start = ((bf16[32,4,1,128]{3,1,2,0:T(4,128)(2,1)}), bf16[32,4,1,128]{3,1,2,0:T(4,128)(2,1)S(1)}, u32[]{:S(2)}, u32[]{:S(2)}) async-start(bf16[32,4,1,128]{3,1,2,0:T(4,128)(2,1)} %bitcast.8), calls=%async_computation | async-start | bytes 65536 | tf_op jit(solution)/shard_map/all_to_all | solution.py:127
  333.9 39.6 %copy-start.12 = (s32[4,2]{1,0:T(4,128)}, s32[4,2]{1,0:T(4,128)S(1)}, u32[]{:S(2)}) copy-start(s32[4,2]{1,0:T(4,128)S(1)} %broadcast_select_fusion.1) | copy-start | bytes 100
  333.9 10.5 copy-start.11
  334.7 42.4 %copy-start.9 = (bf16[4,1,2,4,128]{4,1,3,0,2:T(2,128)(2,1)}, bf16[4,1,2,4,128]{4,1,3,0,2:T(2,128)(2,1)S(1)}, u32[]{:S(2)}) copy-start(bf16[4,1,2,4,128]{4,1,3,0,2:T(2,128)(2,1)S(1)} %stack.16) | copy-start | bytes 24580
  335.8 15.5 %all-to-all-start.2 = ((bf16[32,4,1,2048]{3,1,2,0:T(4,128)(2,1)}), bf16[32,4,1,2048]{3,1,2,0:T(4,128)(2,1)S(1)}, u32[]{:S(2)}, u32[]{:S(2)}) async-start(bf16[32,4,1,2048]{3,1,2,0:T(4,128)(2,1)} %stack.12), calls=%async_computation.2 | async-start | bytes 1048576 | tf_op jit(solution)/shard_map/all_to_all | solution.py:207
  345.4 6.6 copy-start.6
  353.7 15.9 %all-to-all-start.3 = ((bf16[32,4,1,128]{3,1,2,0:T(4,128)(2,1)}), bf16[32,4,1,128]{3,1,2,0:T(4,128)(2,1)S(1)}, u32[]{:S(2)}, u32[]{:S(2)}) async-start(bf16[32,4,1,128]{3,1,2,0:T(4,128)(2,1)} %bitcast.40), calls=%async_computation.3 | async-start | bytes 65536 | tf_op jit(solution)/shard_map/all_to_all | solution.py:127
  364.1 14.0 %copy-start.10 = (bf16[4,1,2,4,128]{4,1,3,0,2:T(2,128)(2,1)}, bf16[4,1,2,4,128]{4,1,3,0,2:T(2,128)(2,1)S(1)}, u32[]{:S(2)}) copy-start(bf16[4,1,2,4,128]{4,1,3,0,2:T(2,128)(2,1)S(1)} %stack.15) | copy-start | bytes 24580
  369.6 16.0 %all-to-all-start.1 = ((bf16[32,4,1,128]{3,1,2,0:T(4,128)(2,1)}), bf16[32,4,1,128]{3,1,2,0:T(4,128)(2,1)S(1)}, u32[]{:S(2)}, u32[]{:S(2)}) async-start(bf16[32,4,1,128]{3,1,2,0:T(4,128)(2,1)} %copy.229), calls=%async_computation.1 | async-start | bytes 65536 | tf_op jit(solution)/shard_map/all_to_all | solution.py:150
  378.2 17.3 %copy-start.5 = (bf16[1,128,2048]{2,1,0:T(8,128)(2,1)S(1)}, bf16[1,128,2048]{2,1,0:T(8,128)(2,1)}, u32[]{:S(2)}) copy-start(bf16[1,128,2048]{2,1,0:T(8,128)(2,1)} %param.22) | copy-start | bytes 1572868
  378.2 30.8 %copy-start.7 = (bf16[4,2,2048]{2,1,0:T(2,128)(2,1)S(1)}, bf16[4,2,2048]{2,1,0:T(2,128)(2,1)}, u32[]{:S(2)}) copy-start(bf16[4,2,2048]{2,1,0:T(2,128)(2,1)} %param.18) | copy-start | bytes 98308
  381.9 603.8 %copy-start.1 = (bf16[1,2048,352]{1,2,0:T(8,128)(2,1)S(1)}, bf16[1,2048,352]{1,2,0:T(8,128)(2,1)}, u32[]{:S(2)}) copy-start(bf16[1,2048,352]{1,2,0:T(8,128)(2,1)} %param.23) | copy-start | bytes 4325380
  385.6 0.6 copy-start.8
  386.2 17.9 %all-to-all-start.4 = ((bf16[32,4,1,128]{3,1,2,0:T(4,128)(2,1)}), bf16[32,4,1,128]{3,1,2,0:T(4,128)(2,1)S(1)}, u32[]{:S(2)}, u32[]{:S(2)}) async-start(bf16[32,4,1,128]{3,1,2,0:T(4,128)(2,1)} %copy.252), calls=%async_computation.4 | async-start | bytes 65536 | tf_op jit(solution)/shard_map/all_to_all | solution.py:150
  395.5 389.2 %all-reduce.14.cloned.1.call-start = ((), (), s32[]{:S(2)}) async-start(), calls=%async_computation.6 | async-start | bytes 2097152
  407.3 941.9 %all-reduce.12.cloned.1.call-start = ((), (), s32[]{:S(2)}) async-start(), calls=%async_computation.5 | async-start | bytes 2097152
  905.7 81.2 %copy-start.4 = (bf16[128,1,2048]{2,1,0:T(2,128)(2,1)}, bf16[128,1,2048]{2,1,0:T(2,128)(2,1)S(1)}, u32[]{:S(2)}) copy-start(bf16[128,1,2048]{2,1,0:T(2,128)(2,1)S(1)} %all_gather.23) | copy-start | bytes 1572868
  985.7 1.3 copy-start.2
  987.0 4.1 copy-start.3
Sparse Core Ops, SparseCore 0:
  407.5 377.1 all-reduce.13
  994.9 354.3 all-reduce.11
